TPU v7x, 256 devices: a whole 4x4x8 slice. The times are simulated.
256 devices in a mesh: view: 16 (over z, core), blk: 16 (over y, x).
Axes of the slice: x: 4, y: 4, z: 8, core: 2. Of those that a mesh axis runs over, the one named last changes fastest.
Arguments:
- estimate: float32 [256, 128, 128], P('blk'), may hold values from 0.5 to 2
- images: bfloat16 [16, 256, 64, 128], P('view', 'blk'), may hold values from 0.5 to 2
- point_spread: float32 [8, 9, 7, 25], replicated, may hold values from 0.01 to 1
- covered: int32 [8, 16, 4], P(None, 'blk'), may hold values from 0 to 1, as said below
Outputs:
- estimate_next: float32 [256, 128, 128], P('blk')
Inputs may be any that keep to these rules, and one draw needn't show every extreme that they name: For each view and each block layer along the first dimension, the covered blocks are consecutive along the second dimension and at most 3; for every view some block layer has exactly 3.
All inputs are finite; a program needn't handle non-finite values.
Results may differ from a plain program's by a relative error of at most 0.0003.
Values may be sent and summed in bfloat16 or wider, within the bound.
A program may use at most 64 MiB of HBM per device.

v0:
```python
import jax
import jax.numpy as jnp
from jax import lax
from jax.sharding import PartitionSpec as P

BY = 32


def with_halo(cells, sides, width):
    for axis, dim in sides:
        count = lax.axis_size(axis)
        ends = count - 1
        head = lax.slice_in_dim(cells, 0, width, axis=dim)
        tail = lax.slice_in_dim(cells, cells.shape[dim] - width, cells.shape[dim], axis=dim)
        cells = jnp.concatenate(
            [
                lax.ppermute(tail, axis, [(i, (i + 1) % count) for i in range(ends)]),
                cells,
                lax.ppermute(head, axis, [((i + 1) % count, i) for i in range(ends)]),
            ],
            axis=dim,
        )
    return cells


def swapped(block, axis, stride):
    count = lax.axis_size(axis)
    route = []
    for low in range(count):
        high = low | 1 << stride
        if high != low and high < count:
            route += [(low, high), (high, low)]
    return lax.ppermute(block, axis, route)


def merged(part, axis, combine):
    gathered = lax.all_gather(part, axis)

    def take(source):
        return lax.dynamic_index_in_dim(gathered, source, 0, False)

    return lax.fori_loop(
        1, lax.axis_size(axis), lambda source, state: combine(state, take(source)), take(0)
    )


def band_table(kernel, depth):
    taps_x, taps_y, taps_z = kernel.shape
    span_z = depth + taps_z - 1
    shape_three = (taps_z, span_z, depth)
    offset = lax.broadcasted_iota(jnp.int32, shape_three, 1) - lax.broadcasted_iota(
        jnp.int32, shape_three, 2
    )
    onehot = (offset == lax.broadcasted_iota(jnp.int32, shape_three, 0)).astype(jnp.bfloat16)
    banded = jnp.einsum("abt,tpz->abpz", kernel, onehot, preferred_element_type=jnp.float32).astype(
        jnp.bfloat16
    )
    inner_width = taps_y * span_z
    padded_width = -(-inner_width // 128) * 128
    banded = banded.reshape(taps_x, inner_width, depth)
    return jnp.pad(banded, ((0, 0), (0, padded_width - inner_width), (0, 0)))


def convolve(padded_part, banded, rows_x, rows_y):
    taps_x = padded_part.shape[0] - rows_x + 1
    taps_y = padded_part.shape[1] - rows_y + 1
    columns = jnp.concatenate(
        [padded_part[:, step_y : step_y + rows_y, :] for step_y in range(taps_y)], axis=2
    )
    columns = jnp.pad(columns, ((0, 0), (0, 0), (0, banded.shape[1] - columns.shape[2])))
    output = None
    for shift_x in range(taps_x):
        partial_sum = jnp.dot(
            columns[shift_x : shift_x + rows_x].reshape(rows_x * rows_y, -1),
            banded[shift_x],
            preferred_element_type=jnp.float32,
        )
        output = partial_sum if output is None else output + partial_sum
    return output.reshape(rows_x, rows_y, -1)


def local(estimate, images, point_spread, covered):
    slab_x, width_y, depth = estimate.shape
    share_w = images.shape[2]
    view_count, taps_x, taps_y, taps_z = point_spread.shape
    rim_x, rim_y, rim_z = ((taps_x - 1) // 2, (taps_y - 1) // 2, (taps_z - 1) // 2)
    shares = width_y // share_w
    share_blocks = share_w // BY
    group = lax.axis_index("view")
    view_id = group // shares
    part = group % shares
    y_start = part * share_w
    source = estimate.astype(jnp.bfloat16)
    rimmed = with_halo(source, (("blk", 0),), rim_x)
    padded = jnp.pad(rimmed, ((0, 0), (rim_y, rim_y), (rim_z, rim_z)))
    spread = lax.dynamic_index_in_dim(point_spread, view_id, 0, keepdims=False)
    kernel = (spread / jnp.sum(spread)).astype(jnp.bfloat16)
    forward = band_table(kernel, depth)
    backward = band_table(kernel[::-1, ::-1, ::-1], depth)
    coverage_row = lax.dynamic_index_in_dim(covered[:, 0, :], view_id, 0, keepdims=False) > 0
    share_cover = lax.dynamic_slice_in_dim(coverage_row, part * share_blocks, share_blocks)
    cell_cover = jnp.repeat(share_cover, BY)[None, :, None]
    image = images[0]
    region = lax.dynamic_slice(
        padded, (0, y_start, 0), (slab_x + 2 * rim_x, share_w + 2 * rim_y, depth + 2 * rim_z)
    )
    blurred = convolve(region, forward, slab_x, share_w)
    quotient = jnp.where(cell_cover, image.astype(jnp.float32) / blurred, 0.0).astype(jnp.bfloat16)
    rim_zeros = jnp.zeros((slab_x, rim_y, depth), jnp.bfloat16)
    edge_rows = jnp.where(part == 0, quotient[:, share_w - rim_y :, :], quotient[:, :rim_y, :])
    partner = swapped(edge_rows, "view", 0)
    lower_rim = jnp.where(part > 0, partner, rim_zeros)
    upper_rim = jnp.where(part < shares - 1, partner, rim_zeros)
    extended = jnp.concatenate([lower_rim, quotient, upper_rim], axis=1)
    quotient_rimmed = with_halo(extended, (("blk", 0),), rim_x)
    padded_quotient = jnp.pad(quotient_rimmed, ((0, 0), (0, 0), (rim_z, rim_z)))
    correction = convolve(padded_quotient, backward, slab_x, share_w)
    share_factor = jnp.where(cell_cover, correction, 1.0)
    n_view = lax.axis_size("view")
    step_x = slab_x // n_view
    rows = share_factor.reshape(n_view, step_x, share_w, depth)
    got = lax.all_to_all(rows, "view", 0, 0)
    got = got.reshape(n_view // shares, shares, step_x, share_w, depth)
    product_rows = jnp.prod(got, axis=0)
    product_rows = jnp.transpose(product_rows, (1, 0, 2, 3)).reshape(step_x, width_y, depth)
    mine = lax.dynamic_slice_in_dim(estimate, group * step_x, step_x, axis=0)
    return lax.all_gather(mine * product_rows, "view", axis=0, tiled=True)


def solution(mesh):
    in_specs = (P("blk", None, None), P("view", "blk", None, None), P(), P(None, "blk", None))
    out_specs = P("blk", None, None)
    return jax.shard_map(local, mesh=mesh, in_specs=in_specs, out_specs=out_specs, check_vma=False)
```

profile of v0, /device:TPU:1, one launch (start us, length us, event | category | flops | bytes accessed | tf_op | source)
XLA Modules:
  0.0 175.8 jit_solution(12433264027804252495)
XLA Ops:
  6.5 1.3 convert_element_type.38
  7.9 4.0 %collective-permute-start = (bf16[4,128,128]{2,1,0:T(8,128)(2,1)S(1)}, bf16[4,128,128]{2,1,0:T(8,128)(2,1)S(1)}, u32[]{:S(2)}, u32[]{:S(2)}) collective-permute-start(bf16[4,128,128]{2,1,0:T(8,128)(2,1)S(1)} %get-tuple-element.40), channel_id=1, source_target_pairs={{0,1},{1,2},{2,3},{3,4},{4,5},{5,6},{6,7},{7,8},{8,9},{9,10},{10,1... | collective-permute-start | bytes 393224 | tf_op jit(solution)/shard_map/ppermute | solution.py:17
  11.8 1.3 collective-permute-start.1
  13.2 1.7 fusion.97
  14.8 3.2 %fusion.10 = bf16[9,7,152,128]{3,1,2,0:T(8,128)(2,1)} fusion(f32[1,9,7,25]{3,0,2,1:T(1,128)S(1)} %get-tuple-element.6, f32[]{:T(128)} %get-tuple-element.5), kind=kOutput, calls=%fused_computation.13 | convolution fusion | flops 63488080 | bytes 2457760 | tf_op jit(solution)/shard_map/abt,tpz->abpz/dot_general | solution.py:55
  18.0 1.6 iota_compare_fusion
  19.6 2.1 %copy.10 = bf16[9,7,152,128]{3,2,1,0:T(8,128)(2,1)S(1)} copy(bf16[9,7,152,128]{3,1,2,0:T(8,128)(2,1)} %fusion.10) | data formatting | bytes 4902912 | tf_op jit(solution)/shard_map/convert_element_type | solution.py:55
  21.8 0.1 fusion.76
  22.1 2.9 %fusion.23 = bf16[24,70,152]{2,1,0:T(8,128)(2,1)S(1)} fusion(s32[]{:T(128)S(6)} %select_n.67, bf16[4,128,128]{2,1,0:T(8,128)(2,1)S(1)} %collective-permute-done, bf16[16,128,128]{2,1,0:T(8,128)(2,1)S(1)} %convert_element_type.38, pred[24,134,152]{2,1,0:T(8,128)(4,1)} %get-tuple-element.45, pred[24,134,152]{2,1,0:T(8,128)(4,1)} %get-tuple-element.46, ...), kind=kLoop, calls=%fused_computation.61 | loop fusion | flops 5873280 | bytes 1808896 | tf_op jit(solution)/shard_map/concatenate | solution.py:15
  25.0 3.1 %fusion.99 = (bf16[24,64,152]{2,1,0:T(8,128)(2,1)S(1)}, bf16[24,64,152]{2,1,0:T(8,128)(2,1)}, bf16[24,64,152]{2,1,0:T(8,128)(2,1)}, bf16[24,64,152]{2,1,0:T(8,12...) fusion(bf16[24,70,152]{2,1,0:T(8,128)(2,1)S(1)} %fusion.23), kind=kLoop, calls=%fused_computation.152 | loop fusion | bytes 6537216 | tf_op jit(solution)/shard_map/slice | solution.py:68
  28.1 8.4 %concatenate.16 = bf16[24,64,1064]{2,1,0:T(8,128)(2,1)} concatenate(bf16[24,64,152]{2,1,0:T(8,128)(2,1)} %get-tuple-element.38, bf16[24,64,152]{2,1,0:T(8,128)(2,1)} %get-tuple-element.37, bf16[24,64,152]{2,1,0:T(8,128)(2,1)} %get-tuple-element.36, bf16[24,64,152]{2,1,0:T(8,128)(2,1)} %get-tuple-element.35, bf16[24,64,152]{2,1,0:T(8,128)(2,1)} %get-tuple-element.34, ...), dimensions={2} | concatenate | bytes 6537216 | tf_op jit(solution)/shard_map/concatenate | solution.py:67
  36.5 12.6 %pad_slice_fusion.27 = (bf16[16,64,1152]{2,1,0:T(8,128)(2,1)S(1)}, bf16[16,64,1152]{2,1,0:T(8,128)(2,1)S(1)}, bf16[16,64,1152]{2,1,0:T(8,128)(2,1)S(1)}, bf16[16...) fusion(bf16[24,64,1064]{2,1,0:T(8,128)(2,1)} %concatenate.16), kind=kLoop, calls=%fused_computation.106 | loop fusion | bytes 24502272 | tf_op jit(solution)/shard_map/slice | solution.py:74
  49.1 0.8 fusion.35
  49.9 0.8 convolution_add_fusion.15
  50.7 0.8 convolution_add_fusion.14
  51.5 0.8 convolution_add_fusion.13
  52.3 0.8 convolution_add_fusion.12
  53.1 0.8 convolution_add_fusion.11
  53.9 0.8 convolution_add_fusion.10
  54.6 0.8 convolution_add_fusion.9
  55.4 0.8 convolution_add_fusion.8
  56.2 0.2 copy-done
  56.4 0.1 fusion.33
  56.6 1.1 collective-permute-start.2
  57.6 0.6 fusion.96
  58.6 1.3 collective-permute-start.4
  59.9 4.9 %collective-permute-start.3 = (bf16[4,70,128]{2,1,0:T(8,128)(2,1)S(1)}, bf16[4,70,128]{2,1,0:T(8,128)(2,1)S(1)}, u32[]{:S(2)}, u32[]{:S(2)}) collective-permute-start(bf16[4,70,128]{2,1,0:T(8,128)(2,1)S(1)} %get-tuple-element.41), channel_id=1, source_target_pairs={{0,1},{1,2},{2,3},{3,4},{4,5},{5,6},{6,7},{7,8},{8,9},{9,10},{10,1... | collective-permute-start | bytes 215048 | tf_op jit(solution)/shard_map/ppermute | solution.py:17
  64.8 1.0 fusion.13
  65.7 0.3 copy.11
  66.1 0.7 select_maximum_fusion
  66.8 3.1 %fusion.98 = (bf16[24,64,152]{2,1,0:T(8,128)(2,1)S(1)}, bf16[24,64,152]{2,1,0:T(8,128)(2,1)}, bf16[24,64,152]{2,1,0:T(8,128)(2,1)}, bf16[24,64,152]{2,1,0:T(8,12...) fusion(bf16[24,70,152]{2,1,0:T(8,128)(2,1)S(1)} %select_maximum_fusion), kind=kLoop, calls=%fused_computation.151 | loop fusion | bytes 6537216 | tf_op jit(solution)/shard_map/slice | solution.py:68
  70.0 8.4 %concatenate.19 = bf16[24,64,1064]{2,1,0:T(8,128)(2,1)} concatenate(bf16[24,64,152]{2,1,0:T(8,128)(2,1)} %get-tuple-element.31, bf16[24,64,152]{2,1,0:T(8,128)(2,1)} %get-tuple-element.30, bf16[24,64,152]{2,1,0:T(8,128)(2,1)} %get-tuple-element.29, bf16[24,64,152]{2,1,0:T(8,128)(2,1)} %get-tuple-element.28, bf16[24,64,152]{2,1,0:T(8,128)(2,1)} %get-tuple-element.27, ...), dimensions={2} | concatenate | bytes 6537216 | tf_op jit(solution)/shard_map/concatenate | solution.py:67
  78.4 12.6 %pad_slice_fusion.18 = (bf16[16,64,1152]{2,1,0:T(8,128)(2,1)S(1)}, bf16[16,64,1152]{2,1,0:T(8,128)(2,1)S(1)}, bf16[16,64,1152]{2,1,0:T(8,128)(2,1)S(1)}, bf16[16...) fusion(bf16[24,64,1064]{2,1,0:T(8,128)(2,1)} %concatenate.19), kind=kLoop, calls=%fused_computation.97 | loop fusion | bytes 24502272 | tf_op jit(solution)/shard_map/slice | solution.py:74
  91.0 0.8 fusion.54
  91.8 0.8 convolution_add_fusion.7
  92.6 0.8 convolution_add_fusion.6
  93.4 0.8 convolution_add_fusion.5
  94.1 0.8 convolution_add_fusion.4
  94.9 0.8 convolution_add_fusion.3
  95.7 0.8 convolution_add_fusion.2
  96.5 0.8 convolution_add_fusion.1
  97.3 0.8 convolution_add_fusion
  98.1 0.9 broadcast_select_fusion
  99.0 9.7 %all-to-all-start = ((f32[16,1,64,128]{3,2,1,0:T(8,128)}), f32[16,1,64,128]{3,2,1,0:T(8,128)S(1)}, u32[]{:S(2)}, u32[]{:S(2)}) async-start(f32[16,1,64,128]{3,2,1,0:T(8,128)} %broadcast_select_fusion), calls=%async_computation | async-start | bytes 1048576 | tf_op jit(solution)/shard_map/all_to_all | solution.py:122
  108.7 17.3 %all-to-all-done = f32[16,1,64,128]{3,2,1,0:T(8,128)S(1)} async-done(((f32[16,1,64,128]{3,2,1,0:T(8,128)}), f32[16,1,64,128]{3,2,1,0:T(8,128)S(1)}, u32[]{:S(2)}, u32[]{:S(2)}) %all-to-all-start) | async-done | bytes 524320 | tf_op jit(solution)/shard_map/all_to_all | solution.py:122
  126.0 1.5 bitcast_multiply_fusion
  127.5 39.1 %all-gather.2.cloned.1.call-done = f32[16,128,128]{2,1,0:T(8,128)} async-done(((f32[1,128,128]{2,1,0:T(8,128)}), f32[16,128,128]{2,1,0:T(8,128)}) %all-gather.2.cloned.1.call-update) | async-done | bytes 1048592 | tf_op jit(solution)/shard_map/all_gather | solution.py:127
  166.7 2.3 %copy.26 = f32[16,128,128]{2,1,0:T(8,128)} copy(f32[16,128,128]{2,1,0:T(8,128)} %all-gather.2.cloned.1.call-done) | data formatting | bytes 2097152
  (19 shorter events, 0.7 us)
Async XLA Ops:
  7.9 14.2 %collective-permute-start = (bf16[4,128,128]{2,1,0:T(8,128)(2,1)S(1)}, bf16[4,128,128]{2,1,0:T(8,128)(2,1)S(1)}, u32[]{:S(2)}, u32[]{:S(2)}) collective-permute-start(bf16[4,128,128]{2,1,0:T(8,128)(2,1)S(1)} %get-tuple-element.40), channel_id=1, source_target_pairs={{0,1},{1,2},{2,3},{3,4},{4,5},{5,6},{6,7},{7,8},{8,9},{9,10},{10,1... | collective-permute-start | bytes 393224 | tf_op jit(solution)/shard_map/ppermute | solution.py:17
  11.8 10.3 %collective-permute-start.1 = (bf16[4,128,128]{2,1,0:T(8,128)(2,1)S(1)}, bf16[4,128,128]{2,1,0:T(8,128)(2,1)S(1)}, u32[]{:S(2)}, u32[]{:S(2)}) collective-permute-start(bf16[4,128,128]{2,1,0:T(8,128)(2,1)S(1)} %get-tuple-element.39), channel_id=1, source_target_pairs={{1,0},{2,1},{3,2},{4,3},{5,4},{6,5},{7,6},{8,7},{9,8},{10,9},{11,1... | collective-permute-start | bytes 393224 | tf_op jit(solution)/shard_map/ppermute | solution.py:19
  19.6 2.2 %copy-start.1 = (s32[8,1,4]{0,2,1:T(4,128)S(1)}, s32[8,1,4]{0,2,1:T(4,128)}, u32[]{:S(2)}) copy-start(s32[8,1,4]{0,2,1:T(4,128)} %param.7) | copy-start | bytes 388
  55.4 1.0 copy-start
  56.6 1.9 %collective-permute-start.2 = (bf16[16,3,128]{2,1,0:T(4,128)(2,1)S(1)}, bf16[16,3,128]{2,1,0:T(4,128)(2,1)S(1)}, u32[]{:S(2)}, u32[]{:S(2)}) collective-permute-start(bf16[16,3,128]{2,1,0:T(4,128)(2,1)S(1)} %slice_select_fusion), channel_id=1, source_target_pairs={{0,16},{16,0},{32,48},{48,32},{64,80},{80,64},{96,112},{112,96},{1... | collective-permute-start | bytes 36872 | tf_op jit(solution)/shard_map/ppermute | solution.py:33
  58.6 7.5 %collective-permute-start.4 = (bf16[4,70,128]{2,1,0:T(8,128)(2,1)S(1)}, bf16[4,70,128]{2,1,0:T(8,128)(2,1)S(1)}, u32[]{:S(2)}, u32[]{:S(2)}) collective-permute-start(bf16[4,70,128]{2,1,0:T(8,128)(2,1)S(1)} %get-tuple-element.42), channel_id=1, source_target_pairs={{1,0},{2,1},{3,2},{4,3},{5,4},{6,5},{7,6},{8,7},{9,8},{10,9},{11,1... | collective-permute-start | bytes 215048 | tf_op jit(solution)/shard_map/ppermute | solution.py:19
  59.9 6.3 %collective-permute-start.3 = (bf16[4,70,128]{2,1,0:T(8,128)(2,1)S(1)}, bf16[4,70,128]{2,1,0:T(8,128)(2,1)S(1)}, u32[]{:S(2)}, u32[]{:S(2)}) collective-permute-start(bf16[4,70,128]{2,1,0:T(8,128)(2,1)S(1)} %get-tuple-element.41), channel_id=1, source_target_pairs={{0,1},{1,2},{2,3},{3,4},{4,5},{5,6},{6,7},{7,8},{8,9},{9,10},{10,1... | collective-permute-start | bytes 215048 | tf_op jit(solution)/shard_map/ppermute | solution.py:17
  99.0 27.0 %all-to-all-start = ((f32[16,1,64,128]{3,2,1,0:T(8,128)}), f32[16,1,64,128]{3,2,1,0:T(8,128)S(1)}, u32[]{:S(2)}, u32[]{:S(2)}) async-start(f32[16,1,64,128]{3,2,1,0:T(8,128)} %broadcast_select_fusion), calls=%async_computation | async-start | bytes 1048576 | tf_op jit(solution)/shard_map/all_to_all | solution.py:122
  108.7 58.0 %all-gather.2.cloned.1.call-start = ((), (), s32[]{:S(2)}) async-start(), calls=%async_computation.1 | async-start | bytes 1114112 | tf_op jit(solution)/shard_map/all_gather | solution.py:127
Sparse Core Ops, SparseCore 0:
  127.7 38.9 all-gather.1
where the time goes:
time: 177 us; the launch traced here: 176 us
  waiting for transfers between devices  56.6 us (32%)
  local copies, waits for them, and re-layouts  53.6 us (30%)
  starting transfers between devices  22.2 us (13%)
  matrix products  18.2 us (10%)
  between operations  13.7 us (8%)
  other arithmetic  11.5 us (6%)
    all_gather x1, waiting for transfers between devices, local(): return lax.all_gather(mine * product_rows, 'view', axis=0, tiled=True)  39.1 us
    slice x2, local copies, waits for them, and re-layouts, convolve(): columns[shift_x:shift_x + rows_x].reshape(rows_x * rows_y, -1)  25.2 us
    all_to_all x1, waiting for transfers between devices, local(): got = lax.all_to_all(rows, 'view', 0, 0)  17.3 us
    concatenate x2, local copies, waits for them, and re-layouts, convolve(): jnp.concatenate([padded_part[:, step_y:step_y + rows_y, :] for step_y in...  16.9 us
    dot_general x18, matrix products, convolve(): jnp.dot(columns[shift_x:shift_x + rows_x].reshape(rows_x * rows_y, -1), b...  14 us
    all_to_all x1, starting transfers between devices, local(): got = lax.all_to_all(rows, 'view', 0, 0)  9.68 us
    ppermute x2, starting transfers between devices, with_halo(): lax.ppermute(tail, axis, [(i, (i + 1) % count) for i in range(ends)])  8.85 us
    slice x2, local copies, waits for them, and re-layouts, convolve(): padded_part[:, step_y:step_y + rows_y, :]  6.25 us
  transfers between devices with their start and end apart: 7, of which 4 were waited for; matrix products, arithmetic and copies ran while one was open for 6% of the time, Pallas kernels for 0%

commit v1 on v0

--- a/solution.py
+++ b/solution.py
@@ -80,6 +80,29 @@
 
 
 def local(estimate, images, point_spread, covered):
+
+    def groups_recast(m):
+        next_value = lax.axis_size("view")
+        front = lax.axis_index("view")
+        arr_out, inter, local_now = (next_value, front, m.shape[0])
+        store = tuple(((c, (c + 1) % arr_out) for c in range(arr_out)))
+        parts_seen = tuple(((c, (c - 1) % arr_out) for c in range(arr_out)))
+        state_now = jnp.zeros((*m.shape[:0], arr_out * local_now, *m.shape[1:]), m.dtype)
+        state_now = lax.dynamic_update_slice_in_dim(state_now, m, inter * local_now, axis=0)
+        local_part = found_now = m
+        met_up = arr_out // 2
+        for rr in range(1, met_up + 1):
+            local_part = lax.ppermute(local_part, "view", perm=store)
+            state_now = lax.dynamic_update_slice_in_dim(
+                state_now, local_part, (inter - rr) % arr_out * local_now, axis=0
+            )
+            if rr < arr_out - met_up:
+                found_now = lax.ppermute(found_now, perm=parts_seen, axis_name="view")
+                state_now = lax.dynamic_update_slice_in_dim(
+                    state_now, found_now, (inter + rr) % arr_out * local_now, axis=0
+                )
+        return state_now
+
     slab_x, width_y, depth = estimate.shape
     share_w = images.shape[2]
     view_count, taps_x, taps_y, taps_z = point_spread.shape
@@ -124,7 +147,7 @@
     product_rows = jnp.prod(got, axis=0)
     product_rows = jnp.transpose(product_rows, (1, 0, 2, 3)).reshape(step_x, width_y, depth)
     mine = lax.dynamic_slice_in_dim(estimate, group * step_x, step_x, axis=0)
-    return lax.all_gather(mine * product_rows, "view", axis=0, tiled=True)
+    return groups_recast(mine * product_rows)
 
 
 def solution(mesh):

time: 177 us -> 166 us (0.938)
  the two profiles are of different devices: /device:TPU:1 before, /device:TPU:6 now
where the time goes in v1:
time: 166 us; the launch traced here: 164 us
  local copies, waits for them, and re-layouts  52.4 us (32%)
  starting transfers between devices  42.6 us (26%)
  waiting for transfers between devices  39.8 us (24%)
  matrix products  18.2 us (11%)
  other arithmetic  11 us (7%)
    slice x2, local copies, waits for them, and re-layouts, convolve(): columns[shift_x:shift_x + rows_x].reshape(rows_x * rows_y, -1)  25.4 us
    ppermute x7, starting transfers between devices, groups_recast(): found_now = lax.ppermute(found_now, perm=parts_seen, axis_name='view')  19 us
    ppermute x8, waiting for transfers between devices, groups_recast(): local_part = lax.ppermute(local_part, 'view', perm=store)  18.2 us
    concatenate x2, local copies, waits for them, and re-layouts, convolve(): jnp.concatenate([padded_part[:, step_y:step_y + rows_y, :] for step_y in...  16.8 us
    all_to_all x1, waiting for transfers between devices, local(): got = lax.all_to_all(rows, 'view', 0, 0)  16 us
    dot_general x18, matrix products, convolve(): jnp.dot(columns[shift_x:shift_x + rows_x].reshape(rows_x * rows_y, -1), b...  14 us
    ppermute x2, starting transfers between devices, with_halo(): lax.ppermute(tail, axis, [(i, (i + 1) % count) for i in range(ends)])  8.91 us
    all_to_all x1, starting transfers between devices, local(): got = lax.all_to_all(rows, 'view', 0, 0)  8.57 us
  transfers between devices with their start and end apart: 21, of which 11 were waited for; matrix products, arithmetic and copies ran while one was open for 7% of the time, Pallas kernels for 0%

profile of v1, /device:TPU:6, one launch (start us, length us, event | category | flops | bytes accessed | tf_op | source)
XLA Modules:
  0.0 164.4 jit_solution(736800878585628629)
XLA Ops:
  0.0 1.3 convert_element_type.38
  1.3 3.4 %collective-permute-start = (bf16[4,128,128]{2,1,0:T(8,128)(2,1)S(1)}, bf16[4,128,128]{2,1,0:T(8,128)(2,1)S(1)}, u32[]{:S(2)}, u32[]{:S(2)}) collective-permute-start(bf16[4,128,128]{2,1,0:T(8,128)(2,1)S(1)} %get-tuple-element.42), channel_id=1, source_target_pairs={{0,1},{1,2},{2,3},{3,4},{4,5},{5,6},{6,7},{7,8},{8,9},{9,10},{10,1... | collective-permute-start | bytes 393224 | tf_op jit(solution)/shard_map/ppermute | solution.py:17
  4.8 2.4 %collective-permute-start.1 = (bf16[4,128,128]{2,1,0:T(8,128)(2,1)S(1)}, bf16[4,128,128]{2,1,0:T(8,128)(2,1)S(1)}, u32[]{:S(2)}, u32[]{:S(2)}) collective-permute-start(bf16[4,128,128]{2,1,0:T(8,128)(2,1)S(1)} %get-tuple-element.41), channel_id=1, source_target_pairs={{1,0},{2,1},{3,2},{4,3},{5,4},{6,5},{7,6},{8,7},{9,8},{10,9},{11,1... | collective-permute-start | bytes 393224 | tf_op jit(solution)/shard_map/ppermute | solution.py:19
  7.2 1.7 %fusion.97 = (f32[]{:T(128)}, f32[1,9,7,25]{3,0,2,1:T(1,128)S(1)}) fusion(f32[8,9,7,25]{3,0,2,1:T(8,128)} %param.6, s32[]{:T(128)S(6)} %select_n.168), kind=kLoop, calls=%fused_computation.166 | loop fusion | flops 1574 | bytes 12608 | tf_op jit(solution)/shard_map/reduce_sum | solution.py:120
  8.9 3.2 %fusion.10 = bf16[9,7,152,128]{3,1,2,0:T(8,128)(2,1)} fusion(f32[1,9,7,25]{3,0,2,1:T(1,128)S(1)} %get-tuple-element.8, f32[]{:T(128)} %get-tuple-element.7), kind=kOutput, calls=%fused_computation.13 | convolution fusion | flops 63488080 | bytes 2457760 | tf_op jit(solution)/shard_map/abt,tpz->abpz/dot_general | solution.py:55
  12.1 1.6 iota_compare_fusion
  13.7 2.1 %copy.10 = bf16[9,7,152,128]{3,2,1,0:T(8,128)(2,1)S(1)} copy(bf16[9,7,152,128]{3,1,2,0:T(8,128)(2,1)} %fusion.10) | data formatting | bytes 4902912 | tf_op jit(solution)/shard_map/convert_element_type | solution.py:55
  16.3 2.9 %fusion.23 = bf16[24,70,152]{2,1,0:T(8,128)(2,1)S(1)} fusion(s32[]{:T(128)S(6)} %select_n.173, bf16[4,128,128]{2,1,0:T(8,128)(2,1)S(1)} %collective-permute-done, bf16[16,128,128]{2,1,0:T(8,128)(2,1)S(1)} %convert_element_type.38, pred[24,134,152]{2,1,0:T(8,128)(4,1)} %get-tuple-element.47, pred[24,134,152]{2,1,0:T(8,128)(4,1)} %get-tuple-element.48, ...), kind=kLoop, calls=%fused_computation.61 | loop fusion | flops 5873280 | bytes 1808896 | tf_op jit(solution)/shard_map/concatenate | solution.py:15
  19.2 3.1 %fusion.99 = (bf16[24,64,152]{2,1,0:T(8,128)(2,1)S(1)}, bf16[24,64,152]{2,1,0:T(8,128)(2,1)}, bf16[24,64,152]{2,1,0:T(8,128)(2,1)}, bf16[24,64,152]{2,1,0:T(8,12...) fusion(bf16[24,70,152]{2,1,0:T(8,128)(2,1)S(1)} %fusion.23), kind=kLoop, calls=%fused_computation.168 | loop fusion | bytes 6537216 | tf_op jit(solution)/shard_map/slice | solution.py:68
  22.3 8.4 %concatenate.16 = bf16[24,64,1064]{2,1,0:T(8,128)(2,1)} concatenate(bf16[24,64,152]{2,1,0:T(8,128)(2,1)} %get-tuple-element.40, bf16[24,64,152]{2,1,0:T(8,128)(2,1)} %get-tuple-element.39, bf16[24,64,152]{2,1,0:T(8,128)(2,1)} %get-tuple-element.38, bf16[24,64,152]{2,1,0:T(8,128)(2,1)} %get-tuple-element.37, bf16[24,64,152]{2,1,0:T(8,128)(2,1)} %get-tuple-element.36, ...), dimensions={2} | concatenate | bytes 6537216 | tf_op jit(solution)/shard_map/concatenate | solution.py:67
  30.7 12.7 %pad_slice_fusion.27 = (bf16[16,64,1152]{2,1,0:T(8,128)(2,1)S(1)}, bf16[16,64,1152]{2,1,0:T(8,128)(2,1)S(1)}, bf16[16,64,1152]{2,1,0:T(8,128)(2,1)S(1)}, bf16[16...) fusion(bf16[24,64,1064]{2,1,0:T(8,128)(2,1)} %concatenate.16), kind=kLoop, calls=%fused_computation.106 | loop fusion | bytes 24502272 | tf_op jit(solution)/shard_map/slice | solution.py:74
  43.4 0.8 fusion.35
  44.2 0.8 convolution_add_fusion.15
  45.0 0.8 convolution_add_fusion.14
  46.5 0.8 convolution_add_fusion.12
  48.9 0.8 convolution_add_fusion.9
  52.2 5.5 %collective-permute-start.3 = (bf16[4,70,128]{2,1,0:T(8,128)(2,1)S(1)}, bf16[4,70,128]{2,1,0:T(8,128)(2,1)S(1)}, u32[]{:S(2)}, u32[]{:S(2)}) collective-permute-start(bf16[4,70,128]{2,1,0:T(8,128)(2,1)S(1)} %get-tuple-element.43), channel_id=1, source_target_pairs={{0,1},{1,2},{2,3},{3,4},{4,5},{5,6},{6,7},{7,8},{8,9},{9,10},{10,1... | collective-permute-start | bytes 215048 | tf_op jit(solution)/shard_map/ppermute | solution.py:17
  57.7 1.9 %collective-permute-start.4 = (bf16[4,70,128]{2,1,0:T(8,128)(2,1)S(1)}, bf16[4,70,128]{2,1,0:T(8,128)(2,1)S(1)}, u32[]{:S(2)}, u32[]{:S(2)}) collective-permute-start(bf16[4,70,128]{2,1,0:T(8,128)(2,1)S(1)} %get-tuple-element.44), channel_id=1, source_target_pairs={{1,0},{2,1},{3,2},{4,3},{5,4},{6,5},{7,6},{8,7},{9,8},{10,9},{11,1... | collective-permute-start | bytes 215048 | tf_op jit(solution)/shard_map/ppermute | solution.py:19
  59.6 1.0 fusion.13
  61.0 5.1 %collective-permute-done.4 = bf16[4,70,128]{2,1,0:T(8,128)(2,1)S(1)} collective-permute-done((bf16[4,70,128]{2,1,0:T(8,128)(2,1)S(1)}, bf16[4,70,128]{2,1,0:T(8,128)(2,1)S(1)}, u32[]{:S(2)}, u32[]{:S(2)}) %collective-permute-start.4) | collective-permute-done | bytes 71712 | tf_op jit(solution)/shard_map/ppermute | solution.py:19
  66.7 3.1 %fusion.98 = (bf16[24,64,152]{2,1,0:T(8,128)(2,1)S(1)}, bf16[24,64,152]{2,1,0:T(8,128)(2,1)}, bf16[24,64,152]{2,1,0:T(8,128)(2,1)}, bf16[24,64,152]{2,1,0:T(8,12...) fusion(bf16[24,70,152]{2,1,0:T(8,128)(2,1)S(1)} %select_maximum_fusion), kind=kLoop, calls=%fused_computation.167 | loop fusion | bytes 6537216 | tf_op jit(solution)/shard_map/slice | solution.py:68
  69.8 8.4 %concatenate.19 = bf16[24,64,1064]{2,1,0:T(8,128)(2,1)} concatenate(bf16[24,64,152]{2,1,0:T(8,128)(2,1)} %get-tuple-element.33, bf16[24,64,152]{2,1,0:T(8,128)(2,1)} %get-tuple-element.32, bf16[24,64,152]{2,1,0:T(8,128)(2,1)} %get-tuple-element.31, bf16[24,64,152]{2,1,0:T(8,128)(2,1)} %get-tuple-element.30, bf16[24,64,152]{2,1,0:T(8,128)(2,1)} %get-tuple-element.29, ...), dimensions={2} | concatenate | bytes 6537216 | tf_op jit(solution)/shard_map/concatenate | solution.py:67
  78.3 12.7 %pad_slice_fusion.18 = (bf16[16,64,1152]{2,1,0:T(8,128)(2,1)S(1)}, bf16[16,64,1152]{2,1,0:T(8,128)(2,1)S(1)}, bf16[16,64,1152]{2,1,0:T(8,128)(2,1)S(1)}, bf16[16...) fusion(bf16[24,64,1064]{2,1,0:T(8,128)(2,1)} %concatenate.19), kind=kLoop, calls=%fused_computation.97 | loop fusion | bytes 24502272 | tf_op jit(solution)/shard_map/slice | solution.py:74
  91.8 0.8 convolution_add_fusion.7
  94.1 0.8 convolution_add_fusion.4
  94.9 0.8 convolution_add_fusion.3
  95.7 0.8 convolution_add_fusion.2
  97.3 0.8 convolution_add_fusion
  98.1 0.9 broadcast_select_fusion
  99.0 8.6 %all-to-all-start = ((f32[16,1,64,128]{3,2,1,0:T(8,128)}), f32[16,1,64,128]{3,2,1,0:T(8,128)S(1)}, u32[]{:S(2)}, u32[]{:S(2)}) async-start(f32[16,1,64,128]{3,2,1,0:T(8,128)} %broadcast_select_fusion), calls=%async_computation | async-start | bytes 1048576 | tf_op jit(solution)/shard_map/all_to_all | solution.py:145
  107.6 16.0 %all-to-all-done = f32[16,1,64,128]{3,2,1,0:T(8,128)S(1)} async-done(((f32[16,1,64,128]{3,2,1,0:T(8,128)}), f32[16,1,64,128]{3,2,1,0:T(8,128)S(1)}, u32[]{:S(2)}, u32[]{:S(2)}) %all-to-all-start) | async-done | bytes 524320 | tf_op jit(solution)/shard_map/all_to_all | solution.py:145
  123.7 0.9 constant_dynamic-update-slice_fusion.15
  124.6 1.7 %collective-permute-start.5 = (f32[1,128,128]{2,1,0:T(8,128)S(1)}, f32[1,128,128]{2,1,0:T(8,128)S(1)}, u32[]{:S(2)}, u32[]{:S(2)}) collective-permute-start(f32[1,128,128]{2,1,0:T(8,128)S(1)} %get-tuple-element.6), channel_id=1, source_target_pairs={{0,16},{16,32},{32,48},{48,64},{64,80},{80,96},{96,112},{112,128},... | collective-permute-start | bytes 196616 | tf_op jit(solution)/shard_map/ppermute | solution.py:95
  126.3 1.3 collective-permute-start.6
  127.5 1.9 %collective-permute-done.5 = f32[1,128,128]{2,1,0:T(8,128)S(1)} collective-permute-done((f32[1,128,128]{2,1,0:T(8,128)S(1)}, f32[1,128,128]{2,1,0:T(8,128)S(1)}, u32[]{:S(2)}, u32[]{:S(2)}) %collective-permute-start.5) | collective-permute-done | bytes 65568 | tf_op jit(solution)/shard_map/ppermute | solution.py:95
  129.5 3.0 %collective-permute-start.8 = (f32[1,128,128]{2,1,0:T(8,128)S(1)}, f32[1,128,128]{2,1,0:T(8,128)S(1)}, u32[]{:S(2)}, u32[]{:S(2)}) collective-permute-start(f32[1,128,128]{2,1,0:T(8,128)S(1)} %collective-permute-done.6), channel_id=1, source_target_pairs={{0,240},{16,0},{32,16},{48,32},{64,48},{80,64},{96,80},{112,96},{1... | collective-permute-start | bytes 196616 | tf_op jit(solution)/shard_map/ppermute | solution.py:100
  132.5 1.9 %collective-permute-done.7 = f32[1,128,128]{2,1,0:T(8,128)S(1)} collective-permute-done((f32[1,128,128]{2,1,0:T(8,128)S(1)}, f32[1,128,128]{2,1,0:T(8,128)S(1)}, u32[]{:S(2)}, u32[]{:S(2)}) %collective-permute-start.7) | collective-permute-done | bytes 65568 | tf_op jit(solution)/shard_map/ppermute | solution.py:95
  134.4 3.0 %collective-permute-start.10 = (f32[1,128,128]{2,1,0:T(8,128)S(1)}, f32[1,128,128]{2,1,0:T(8,128)S(1)}, u32[]{:S(2)}, u32[]{:S(2)}) collective-permute-start(f32[1,128,128]{2,1,0:T(8,128)S(1)} %collective-permute-done.8), channel_id=1, source_target_pairs={{0,240},{16,0},{32,16},{48,32},{64,48},{80,64},{96,80},{112,96},{1... | collective-permute-start | bytes 196616 | tf_op jit(solution)/shard_map/ppermute | solution.py:100
  137.4 1.9 %collective-permute-done.9 = f32[1,128,128]{2,1,0:T(8,128)S(1)} collective-permute-done((f32[1,128,128]{2,1,0:T(8,128)S(1)}, f32[1,128,128]{2,1,0:T(8,128)S(1)}, u32[]{:S(2)}, u32[]{:S(2)}) %collective-permute-start.9) | collective-permute-done | bytes 65568 | tf_op jit(solution)/shard_map/ppermute | solution.py:95
  139.3 3.0 %collective-permute-start.12 = (f32[1,128,128]{2,1,0:T(8,128)S(1)}, f32[1,128,128]{2,1,0:T(8,128)S(1)}, u32[]{:S(2)}, u32[]{:S(2)}) collective-permute-start(f32[1,128,128]{2,1,0:T(8,128)S(1)} %collective-permute-done.10), channel_id=1, source_target_pairs={{0,240},{16,0},{32,16},{48,32},{64,48},{80,64},{96,80},{112,96},{1... | collective-permute-start | bytes 196616 | tf_op jit(solution)/shard_map/ppermute | solution.py:100
  142.3 1.9 %collective-permute-done.11 = f32[1,128,128]{2,1,0:T(8,128)S(1)} collective-permute-done((f32[1,128,128]{2,1,0:T(8,128)S(1)}, f32[1,128,128]{2,1,0:T(8,128)S(1)}, u32[]{:S(2)}, u32[]{:S(2)}) %collective-permute-start.11) | collective-permute-done | bytes 65568 | tf_op jit(solution)/shard_map/ppermute | solution.py:95
  144.2 3.0 %collective-permute-start.14 = (f32[1,128,128]{2,1,0:T(8,128)S(1)}, f32[1,128,128]{2,1,0:T(8,128)S(1)}, u32[]{:S(2)}, u32[]{:S(2)}) collective-permute-start(f32[1,128,128]{2,1,0:T(8,128)S(1)} %collective-permute-done.12), channel_id=1, source_target_pairs={{0,240},{16,0},{32,16},{48,32},{64,48},{80,64},{96,80},{112,96},{1... | collective-permute-start | bytes 196616 | tf_op jit(solution)/shard_map/ppermute | solution.py:100
  147.2 1.9 %collective-permute-done.13 = f32[1,128,128]{2,1,0:T(8,128)S(1)} collective-permute-done((f32[1,128,128]{2,1,0:T(8,128)S(1)}, f32[1,128,128]{2,1,0:T(8,128)S(1)}, u32[]{:S(2)}, u32[]{:S(2)}) %collective-permute-start.13) | collective-permute-done | bytes 65568 | tf_op jit(solution)/shard_map/ppermute | solution.py:95
  149.1 3.0 %collective-permute-start.16 = (f32[1,128,128]{2,1,0:T(8,128)S(1)}, f32[1,128,128]{2,1,0:T(8,128)S(1)}, u32[]{:S(2)}, u32[]{:S(2)}) collective-permute-start(f32[1,128,128]{2,1,0:T(8,128)S(1)} %collective-permute-done.14), channel_id=1, source_target_pairs={{0,240},{16,0},{32,16},{48,32},{64,48},{80,64},{96,80},{112,96},{1... | collective-permute-start | bytes 196616 | tf_op jit(solution)/shard_map/ppermute | solution.py:100
  152.1 1.9 %collective-permute-done.15 = f32[1,128,128]{2,1,0:T(8,128)S(1)} collective-permute-done((f32[1,128,128]{2,1,0:T(8,128)S(1)}, f32[1,128,128]{2,1,0:T(8,128)S(1)}, u32[]{:S(2)}, u32[]{:S(2)}) %collective-permute-start.15) | collective-permute-done | bytes 65568 | tf_op jit(solution)/shard_map/ppermute | solution.py:95
  154.0 3.0 %collective-permute-start.18 = (f32[1,128,128]{2,1,0:T(8,128)S(1)}, f32[1,128,128]{2,1,0:T(8,128)S(1)}, u32[]{:S(2)}, u32[]{:S(2)}) collective-permute-start(f32[1,128,128]{2,1,0:T(8,128)S(1)} %collective-permute-done.16), channel_id=1, source_target_pairs={{0,240},{16,0},{32,16},{48,32},{64,48},{80,64},{96,80},{112,96},{1... | collective-permute-start | bytes 196616 | tf_op jit(solution)/shard_map/ppermute | solution.py:100
  157.0 1.9 %collective-permute-done.17 = f32[1,128,128]{2,1,0:T(8,128)S(1)} collective-permute-done((f32[1,128,128]{2,1,0:T(8,128)S(1)}, f32[1,128,128]{2,1,0:T(8,128)S(1)}, u32[]{:S(2)}, u32[]{:S(2)}) %collective-permute-start.17) | collective-permute-done | bytes 65568 | tf_op jit(solution)/shard_map/ppermute | solution.py:95
  159.0 4.8 %collective-permute-done.19 = f32[1,128,128]{2,1,0:T(8,128)S(1)} collective-permute-done((f32[1,128,128]{2,1,0:T(8,128)S(1)}, f32[1,128,128]{2,1,0:T(8,128)S(1)}, u32[]{:S(2)}, u32[]{:S(2)}) %collective-permute-start.19) | collective-permute-done | bytes 65568 | tf_op jit(solution)/shard_map/ppermute | solution.py:95
  (63 shorter events, 10.2 us)
Async XLA Ops:
  1.3 14.9 %collective-permute-start = (bf16[4,128,128]{2,1,0:T(8,128)(2,1)S(1)}, bf16[4,128,128]{2,1,0:T(8,128)(2,1)S(1)}, u32[]{:S(2)}, u32[]{:S(2)}) collective-permute-start(bf16[4,128,128]{2,1,0:T(8,128)(2,1)S(1)} %get-tuple-element.42), channel_id=1, source_target_pairs={{0,1},{1,2},{2,3},{3,4},{4,5},{5,6},{6,7},{7,8},{8,9},{9,10},{10,1... | collective-permute-start | bytes 393224 | tf_op jit(solution)/shard_map/ppermute | solution.py:17
  4.8 11.5 %collective-permute-start.1 = (bf16[4,128,128]{2,1,0:T(8,128)(2,1)S(1)}, bf16[4,128,128]{2,1,0:T(8,128)(2,1)S(1)}, u32[]{:S(2)}, u32[]{:S(2)}) collective-permute-start(bf16[4,128,128]{2,1,0:T(8,128)(2,1)S(1)} %get-tuple-element.41), channel_id=1, source_target_pairs={{1,0},{2,1},{3,2},{4,3},{5,4},{6,5},{7,6},{8,7},{9,8},{10,9},{11,1... | collective-permute-start | bytes 393224 | tf_op jit(solution)/shard_map/ppermute | solution.py:19
  13.7 2.2 %copy-start.2 = (s32[8,1,4]{0,2,1:T(4,128)S(1)}, s32[8,1,4]{0,2,1:T(4,128)}, u32[]{:S(2)}) copy-start(s32[8,1,4]{0,2,1:T(4,128)} %param.7) | copy-start | bytes 388
  49.7 1.0 copy-start.1
  50.8 1.3 collective-permute-start.2
  52.2 8.8 %collective-permute-start.3 = (bf16[4,70,128]{2,1,0:T(8,128)(2,1)S(1)}, bf16[4,70,128]{2,1,0:T(8,128)(2,1)S(1)}, u32[]{:S(2)}, u32[]{:S(2)}) collective-permute-start(bf16[4,70,128]{2,1,0:T(8,128)(2,1)S(1)} %get-tuple-element.43), channel_id=1, source_target_pairs={{0,1},{1,2},{2,3},{3,4},{4,5},{5,6},{6,7},{7,8},{8,9},{9,10},{10,1... | collective-permute-start | bytes 215048 | tf_op jit(solution)/shard_map/ppermute | solution.py:17
  57.7 8.4 %collective-permute-start.4 = (bf16[4,70,128]{2,1,0:T(8,128)(2,1)S(1)}, bf16[4,70,128]{2,1,0:T(8,128)(2,1)S(1)}, u32[]{:S(2)}, u32[]{:S(2)}) collective-permute-start(bf16[4,70,128]{2,1,0:T(8,128)(2,1)S(1)} %get-tuple-element.44), channel_id=1, source_target_pairs={{1,0},{2,1},{3,2},{4,3},{5,4},{6,5},{7,6},{8,7},{9,8},{10,9},{11,1... | collective-permute-start | bytes 215048 | tf_op jit(solution)/shard_map/ppermute | solution.py:19
  99.0 24.6 %all-to-all-start = ((f32[16,1,64,128]{3,2,1,0:T(8,128)}), f32[16,1,64,128]{3,2,1,0:T(8,128)S(1)}, u32[]{:S(2)}, u32[]{:S(2)}) async-start(f32[16,1,64,128]{3,2,1,0:T(8,128)} %broadcast_select_fusion), calls=%async_computation | async-start | bytes 1048576 | tf_op jit(solution)/shard_map/all_to_all | solution.py:145
  124.6 4.9 %collective-permute-start.5 = (f32[1,128,128]{2,1,0:T(8,128)S(1)}, f32[1,128,128]{2,1,0:T(8,128)S(1)}, u32[]{:S(2)}, u32[]{:S(2)}) collective-permute-start(f32[1,128,128]{2,1,0:T(8,128)S(1)} %get-tuple-element.6), channel_id=1, source_target_pairs={{0,16},{16,32},{32,48},{48,64},{64,80},{80,96},{96,112},{112,128},... | collective-permute-start | bytes 196616 | tf_op jit(solution)/shard_map/ppermute | solution.py:95
  126.3 3.2 %collective-permute-start.6 = (f32[1,128,128]{2,1,0:T(8,128)S(1)}, f32[1,128,128]{2,1,0:T(8,128)S(1)}, u32[]{:S(2)}, u32[]{:S(2)}) collective-permute-start(f32[1,128,128]{2,1,0:T(8,128)S(1)} %get-tuple-element.6), channel_id=1, source_target_pairs={{0,240},{16,0},{32,16},{48,32},{64,48},{80,64},{96,80},{112,96},{1... | collective-permute-start | bytes 196616 | tf_op jit(solution)/shard_map/ppermute | solution.py:100
  129.5 4.9 %collective-permute-start.7 = (f32[1,128,128]{2,1,0:T(8,128)S(1)}, f32[1,128,128]{2,1,0:T(8,128)S(1)}, u32[]{:S(2)}, u32[]{:S(2)}) collective-permute-start(f32[1,128,128]{2,1,0:T(8,128)S(1)} %collective-permute-done.5), channel_id=1, source_target_pairs={{0,16},{16,32},{32,48},{48,64},{64,80},{80,96},{96,112},{112,128},... | collective-permute-start | bytes 196616 | tf_op jit(solution)/shard_map/ppermute | solution.py:95
  129.5 4.9 %collective-permute-start.8 = (f32[1,128,128]{2,1,0:T(8,128)S(1)}, f32[1,128,128]{2,1,0:T(8,128)S(1)}, u32[]{:S(2)}, u32[]{:S(2)}) collective-permute-start(f32[1,128,128]{2,1,0:T(8,128)S(1)} %collective-permute-done.6), channel_id=1, source_target_pairs={{0,240},{16,0},{32,16},{48,32},{64,48},{80,64},{96,80},{112,96},{1... | collective-permute-start | bytes 196616 | tf_op jit(solution)/shard_map/ppermute | solution.py:100
  134.4 4.9 %collective-permute-start.9 = (f32[1,128,128]{2,1,0:T(8,128)S(1)}, f32[1,128,128]{2,1,0:T(8,128)S(1)}, u32[]{:S(2)}, u32[]{:S(2)}) collective-permute-start(f32[1,128,128]{2,1,0:T(8,128)S(1)} %collective-permute-done.7), channel_id=1, source_target_pairs={{0,16},{16,32},{32,48},{48,64},{64,80},{80,96},{96,112},{112,128},... | collective-permute-start | bytes 196616 | tf_op jit(solution)/shard_map/ppermute | solution.py:95
  134.4 4.9 %collective-permute-start.10 = (f32[1,128,128]{2,1,0:T(8,128)S(1)}, f32[1,128,128]{2,1,0:T(8,128)S(1)}, u32[]{:S(2)}, u32[]{:S(2)}) collective-permute-start(f32[1,128,128]{2,1,0:T(8,128)S(1)} %collective-permute-done.8), channel_id=1, source_target_pairs={{0,240},{16,0},{32,16},{48,32},{64,48},{80,64},{96,80},{112,96},{1... | collective-permute-start | bytes 196616 | tf_op jit(solution)/shard_map/ppermute | solution.py:100
  139.3 4.9 %collective-permute-start.11 = (f32[1,128,128]{2,1,0:T(8,128)S(1)}, f32[1,128,128]{2,1,0:T(8,128)S(1)}, u32[]{:S(2)}, u32[]{:S(2)}) collective-permute-start(f32[1,128,128]{2,1,0:T(8,128)S(1)} %collective-permute-done.9), channel_id=1, source_target_pairs={{0,16},{16,32},{32,48},{48,64},{64,80},{80,96},{96,112},{112,128},... | collective-permute-start | bytes 196616 | tf_op jit(solution)/shard_map/ppermute | solution.py:95
  139.3 4.9 %collective-permute-start.12 = (f32[1,128,128]{2,1,0:T(8,128)S(1)}, f32[1,128,128]{2,1,0:T(8,128)S(1)}, u32[]{:S(2)}, u32[]{:S(2)}) collective-permute-start(f32[1,128,128]{2,1,0:T(8,128)S(1)} %collective-permute-done.10), channel_id=1, source_target_pairs={{0,240},{16,0},{32,16},{48,32},{64,48},{80,64},{96,80},{112,96},{1... | collective-permute-start | bytes 196616 | tf_op jit(solution)/shard_map/ppermute | solution.py:100
  144.2 4.9 %collective-permute-start.13 = (f32[1,128,128]{2,1,0:T(8,128)S(1)}, f32[1,128,128]{2,1,0:T(8,128)S(1)}, u32[]{:S(2)}, u32[]{:S(2)}) collective-permute-start(f32[1,128,128]{2,1,0:T(8,128)S(1)} %collective-permute-done.11), channel_id=1, source_target_pairs={{0,16},{16,32},{32,48},{48,64},{64,80},{80,96},{96,112},{112,128},... | collective-permute-start | bytes 196616 | tf_op jit(solution)/shard_map/ppermute | solution.py:95
  144.2 4.9 %collective-permute-start.14 = (f32[1,128,128]{2,1,0:T(8,128)S(1)}, f32[1,128,128]{2,1,0:T(8,128)S(1)}, u32[]{:S(2)}, u32[]{:S(2)}) collective-permute-start(f32[1,128,128]{2,1,0:T(8,128)S(1)} %collective-permute-done.12), channel_id=1, source_target_pairs={{0,240},{16,0},{32,16},{48,32},{64,48},{80,64},{96,80},{112,96},{1... | collective-permute-start | bytes 196616 | tf_op jit(solution)/shard_map/ppermute | solution.py:100
  149.1 4.9 %collective-permute-start.15 = (f32[1,128,128]{2,1,0:T(8,128)S(1)}, f32[1,128,128]{2,1,0:T(8,128)S(1)}, u32[]{:S(2)}, u32[]{:S(2)}) collective-permute-start(f32[1,128,128]{2,1,0:T(8,128)S(1)} %collective-permute-done.13), channel_id=1, source_target_pairs={{0,16},{16,32},{32,48},{48,64},{64,80},{80,96},{96,112},{112,128},... | collective-permute-start | bytes 196616 | tf_op jit(solution)/shard_map/ppermute | solution.py:95
  149.1 4.9 %collective-permute-start.16 = (f32[1,128,128]{2,1,0:T(8,128)S(1)}, f32[1,128,128]{2,1,0:T(8,128)S(1)}, u32[]{:S(2)}, u32[]{:S(2)}) collective-permute-start(f32[1,128,128]{2,1,0:T(8,128)S(1)} %collective-permute-done.14), channel_id=1, source_target_pairs={{0,240},{16,0},{32,16},{48,32},{64,48},{80,64},{96,80},{112,96},{1... | collective-permute-start | bytes 196616 | tf_op jit(solution)/shard_map/ppermute | solution.py:100
  154.0 4.9 %collective-permute-start.17 = (f32[1,128,128]{2,1,0:T(8,128)S(1)}, f32[1,128,128]{2,1,0:T(8,128)S(1)}, u32[]{:S(2)}, u32[]{:S(2)}) collective-permute-start(f32[1,128,128]{2,1,0:T(8,128)S(1)} %collective-permute-done.15), channel_id=1, source_target_pairs={{0,16},{16,32},{32,48},{48,64},{64,80},{80,96},{96,112},{112,128},... | collective-permute-start | bytes 196616 | tf_op jit(solution)/shard_map/ppermute | solution.py:95
  154.0 4.9 %collective-permute-start.18 = (f32[1,128,128]{2,1,0:T(8,128)S(1)}, f32[1,128,128]{2,1,0:T(8,128)S(1)}, u32[]{:S(2)}, u32[]{:S(2)}) collective-permute-start(f32[1,128,128]{2,1,0:T(8,128)S(1)} %collective-permute-done.16), channel_id=1, source_target_pairs={{0,240},{16,0},{32,16},{48,32},{64,48},{80,64},{96,80},{112,96},{1... | collective-permute-start | bytes 196616 | tf_op jit(solution)/shard_map/ppermute | solution.py:100
  158.9 4.9 %collective-permute-start.19 = (f32[1,128,128]{2,1,0:T(8,128)S(1)}, f32[1,128,128]{2,1,0:T(8,128)S(1)}, u32[]{:S(2)}, u32[]{:S(2)}) collective-permute-start(f32[1,128,128]{2,1,0:T(8,128)S(1)} %collective-permute-done.17), channel_id=1, source_target_pairs={{0,16},{16,32},{32,48},{48,64},{64,80},{80,96},{96,112},{112,128},... | collective-permute-start | bytes 196616 | tf_op jit(solution)/shard_map/ppermute | solution.py:95
  159.0 4.9 %copy-start = (f32[16,128,128]{2,1,0:T(8,128)}, f32[16,128,128]{2,1,0:T(8,128)S(1)}, u32[]{:S(2)}) copy-start(f32[16,128,128]{2,1,0:T(8,128)S(1)} %constant_dynamic-update-slice_fusion.1) | copy-start | bytes 3145732
